TPU v7x, 512 devices: a whole 4x8x8 slice. The times are simulated.
512 devices in a mesh: row: 32 (over x, y), col: 16 (over z, core).
Axes of the slice: x: 4, y: 8, z: 8, core: 2. Of those that a mesh axis runs over, the one named last changes fastest.
Arguments:
- item_factors: bfloat16 [64, 2048, 256], P('col', 'row'), may hold values from -1 to 1
- tile_counts: int32 [64], P('col'), may hold values from 1024 to 2048, as said below
- observed_tiles: int32 [32, 32], P('row', 'col'), may hold values from 0 to 3, as said below
- mask_words: int32 [4096, 32, 256], P('row', 'col'), may hold values from 0 to 255
- confidence: float32 [4096], P('row'), may hold values from 1 to 40
- previous: bfloat16 [4096, 256], P('row'), may hold values from -6 to 6
Outputs:
- user_factors: float32 [4096, 256], P('row')
Inputs may be any that keep to these rules, and one draw needn't show every extreme that they name: `tile_counts`: a tile's slots at and past its count are padding; some tile of the draw has all 2048 slots valid. `observed_tiles`: the 2 entries of one user block and one column group are distinct.
All inputs are finite; a program needn't handle non-finite values.
Results may differ from a plain program's by a relative error of at most 0.0013.
The roundings to bfloat16 on the way count: a program that leaves them out, or rounds other values in their place, can miss the bound.
Values may be sent and summed in bfloat16 or wider, within the bound.
A program may use at most 64 MiB of HBM per device.

v0:
```python
import jax
import jax.numpy as jnp
from jax import lax
from jax.sharding import PartitionSpec as P

R = 256
OBS = 2
ITERS = 3


ridge_weight = 0.1


def unpack_bits(words):
    shifts = jnp.arange(8, dtype=jnp.int32)
    bits = jnp.right_shift(words[..., None], shifts) & 1
    return bits.reshape(words.shape[:-1] + (words.shape[-1] * 8,))


def local(item_factors, tile_counts, observed_tiles, mask_words, confidence, previous):
    local_rows = item_factors.shape[1]
    tiles = lax.all_gather(item_factors, "row", axis=1, tiled=True)
    tile_len = tiles.shape[1]
    valid = jnp.arange(tile_len, dtype=jnp.int32)[None, :] < tile_counts[:, None]
    first = lax.axis_index("row") * local_rows
    local_valid = (first + jnp.arange(local_rows, dtype=jnp.int32))[None, :] < tile_counts[:, None]
    masked = jnp.where(local_valid[..., None], item_factors, jnp.zeros_like(item_factors)).reshape(
        -1, R
    )
    gram = lax.psum(
        jnp.einsum("jr,js->rs", masked, masked, preferred_element_type=jnp.float32), ("row", "col")
    )
    picked = observed_tiles[0]
    slot_tiles = tiles[picked]
    seen = (unpack_bits(mask_words) * valid[picked][None].astype(jnp.int32)).astype(jnp.bfloat16)
    seen = jnp.transpose(seen, (1, 0, 2))
    users = previous.shape[0]

    def weighted(rounded):
        total = jnp.zeros((users, R), jnp.float32)
        for slot in range(OBS):
            scores = jnp.einsum(
                "ur,jr->uj", rounded, slot_tiles[slot], preferred_element_type=jnp.float32
            )
            weights = (confidence[:, None] * seen[slot].astype(jnp.float32) * scores).astype(
                jnp.bfloat16
            )
            total = total + jnp.dot(weights, slot_tiles[slot], preferred_element_type=jnp.float32)
        return total

    rhs_part = jnp.zeros((users, R), jnp.float32)
    for slot in range(OBS):
        rhs_part = rhs_part + jnp.dot(
            seen[slot], slot_tiles[slot], preferred_element_type=jnp.float32
        )

    def local_op(vector, summed):
        return (
            jnp.dot(vector, gram, precision=lax.Precision.HIGHEST) + ridge_weight * vector + summed
        )

    def reduce_terms(parts):
        return lax.psum(parts, "col")

    solution = previous.astype(jnp.float32)
    rhs_sum, start_sum = reduce_terms((rhs_part, weighted(previous)))
    rhs = (1.0 + confidence)[:, None] * rhs_sum
    residual = rhs - local_op(solution, start_sum)
    direction = residual
    norm_now = jnp.sum(residual * residual, axis=1)
    for iteration in range(ITERS):
        image = local_op(direction, reduce_terms((weighted(direction.astype(jnp.bfloat16)),))[0])
        step_size = norm_now / jnp.sum(direction * image, axis=1)
        solution = solution + step_size[:, None] * direction
        residual = residual - step_size[:, None] * image
        norm_next = jnp.sum(residual * residual, axis=1)
        direction = residual + (norm_next / norm_now)[:, None] * direction
        norm_now = norm_next
    return solution


def solution(mesh):
    return jax.shard_map(
        local,
        mesh=mesh,
        in_specs=(
            P("col", "row", None),
            P("col"),
            P("row", "col"),
            P("row", "col", None),
            P("row"),
            P("row", None),
        ),
        out_specs=P("row", None),
        check_vma=False,
    )
```

profile of v0, /device:TPU:1, one launch (start us, length us, event | category | flops | bytes accessed | tf_op | source)
XLA Modules:
  0.0 783.4 jit_solution(2195536796156909677)
XLA Ops:
  8.9 2.0 convolution_bitcast_fusion.2
  13.0 1.1 copy.9
  14.2 1.2 fusion.33
  15.5 84.8 %all-gather.2.cloned.1.call-done = bf16[4,2048,256]{2,1,0:T(8,128)(2,1)} async-done(((bf16[4,64,256]{2,1,0:T(8,128)(2,1)}), bf16[4,2048,256]{2,1,0:T(8,128)(2,1)}) %all-gather.2.cloned.1.call-update) | async-done | bytes 4194320 | tf_op jit(solution)/shard_map/all_gather | solution.py:22
  100.3 2.9 gather_fusion.1
  103.5 0.8 fusion.13
  104.3 1.5 fusion.31
  105.8 1.0 convolution_add_fusion.3
  106.9 187.4 %all-reduce.7.cloned.1.call-done = f32[256,256]{1,0:T(8,128)} async-done(((f32[256,256]{1,0:T(8,128)}), f32[256,256]{1,0:T(8,128)}) %all-reduce.7.cloned.1.call-update) | async-done | bytes 262160 | tf_op jit(solution)/shard_map/psum | solution.py:30
  294.3 114.9 %all-reduce.15.cloned.1.call-done = (f32[128,256]{1,0:T(8,128)}, f32[128,256]{1,0:T(8,128)}) async-done(((f32[128,256]{1,0:T(8,128)}, f32[128,256]{1,0:T(8,128)}), (f32[128,256]{1,0:T(8,128)}, f32[128,256]{1,0:T(8,128)})) %all-reduce.15.cloned.1.call-update) | async-done | bytes 262160 | tf_op jit(solution)/shard_map/psum | solution.py:63
  409.1 1.3 fusion.27
  410.4 1.5 fusion.19
  411.9 2.4 fusion.28
  414.4 115.6 %all-reduce.9.cloned.1.call-done = f32[128,256]{1,0:T(8,128)} async-done(((f32[128,256]{1,0:T(8,128)}), f32[128,256]{1,0:T(8,128)}) %all-reduce.9.cloned.1.call-update) | async-done | bytes 131088 | tf_op jit(solution)/shard_map/psum | solution.py:63
  530.0 1.3 multiply_reduce_fusion.3
  531.6 1.9 fusion.17
  533.4 2.5 fusion.29
  536.0 115.8 %all-reduce.11.cloned.1.call-done = f32[128,256]{1,0:T(8,128)} async-done(((f32[128,256]{1,0:T(8,128)}), f32[128,256]{1,0:T(8,128)}) %all-reduce.11.cloned.1.call-update) | async-done | bytes 131088 | tf_op jit(solution)/shard_map/psum | solution.py:63
  651.8 1.3 multiply_reduce_fusion.1
  653.4 1.9 fusion.15
  655.3 2.5 fusion.30
  657.9 115.8 %all-reduce.13.cloned.1.call-done = f32[128,256]{1,0:T(8,128)} async-done(((f32[128,256]{1,0:T(8,128)}), f32[128,256]{1,0:T(8,128)}) %all-reduce.13.cloned.1.call-update) | async-done | bytes 131088 | tf_op jit(solution)/shard_map/psum | solution.py:63
  773.7 1.3 fusion.32
  775.0 0.8 fusion.44
  (42 shorter events, 4.8 us)
Async XLA Ops:
  7.4 92.9 %all-gather.2.cloned.1.call-start = ((), (), s32[]{:S(2)}) async-start(), calls=%async_computation | async-start | bytes 4325376 | tf_op jit(solution)/shard_map/all_gather | solution.py:22
  8.1 286.2 %all-reduce.7.cloned.1.call-start = ((), (), s32[]{:S(2)}) async-start(), calls=%async_computation.1 | async-start | bytes 524288 | tf_op jit(solution)/shard_map/psum | solution.py:30
  10.9 398.2 %all-reduce.15.cloned.1.call-start = ((), (), s32[]{:S(2)}) async-start(), calls=%async_computation.5 | async-start | bytes 524288 | tf_op jit(solution)/shard_map/psum | solution.py:63
  15.4 396.5 %copy-start.1 = (bf16[2,128,2048]{1,2,0:T(8,128)(2,1)}, bf16[2,128,2048]{1,2,0:T(8,128)(2,1)S(1)}, u32[]{:S(2)}) copy-start(bf16[2,128,2048]{1,2,0:T(8,128)(2,1)S(1)} %fusion.33) | copy-start | bytes 3145732
  15.4 88.1 %copy-start.2 = (bf16[128,256]{1,0:T(8,128)(2,1)S(1)}, bf16[128,256]{1,0:T(8,128)(2,1)}, u32[]{:S(2)}) copy-start(bf16[128,256]{1,0:T(8,128)(2,1)} %param.11) | copy-start | bytes 196612
  15.5 88.1 %copy-start.4 = (f32[128]{0:T(128)S(1)}, f32[128]{0:T(128)}, u32[]{:S(2)}) copy-start(f32[128]{0:T(128)} %param.10) | copy-start | bytes 1540
  106.9 423.1 %all-reduce.9.cloned.1.call-start = ((), (), s32[]{:S(2)}) async-start(), calls=%async_computation.2 | async-start | bytes 262144 | tf_op jit(solution)/shard_map/psum | solution.py:63
  411.9 118.1 %copy-start = (f32[256,256]{1,0:T(8,128)S(1)}, f32[256,256]{1,0:T(8,128)}, u32[]{:S(2)}) copy-start(f32[256,256]{1,0:T(8,128)} %all-reduce.7.cloned.1.call-done) | copy-start | bytes 786436
  414.4 237.5 %all-reduce.11.cloned.1.call-start = ((), (), s32[]{:S(2)}) async-start(), calls=%async_computation.3 | async-start | bytes 262144 | tf_op jit(solution)/shard_map/psum | solution.py:63
  536.0 237.7 %all-reduce.13.cloned.1.call-start = ((), (), s32[]{:S(2)}) async-start(), calls=%async_computation.4 | async-start | bytes 262144 | tf_op jit(solution)/shard_map/psum | solution.py:63
  655.3 119.7 %copy-start.3 = (bf16[128,256]{1,0:T(8,128)(2,1)S(1)}, bf16[128,256]{1,0:T(8,128)(2,1)}, u32[]{:S(2)}) copy-start(bf16[128,256]{1,0:T(8,128)(2,1)} %param.11) | copy-start | bytes 196612
Sparse Core Ops, SparseCore 0:
  11.3 88.9 all-gather.1
Sparse Core Ops, SparseCore 1:
  13.6 280.7 all-reduce.6
  296.5 112.6 all-reduce.14
  414.4 115.5 all-reduce.8
  536.1 115.7 all-reduce.10
  657.9 115.7 all-reduce.12
where the time goes:
time: 784 us; the launch traced here: 783 us
  waiting for transfers between devices  735 us (94%)
  matrix products  23.4 us (3%)
  between operations  15.3 us (2%)
    psum x4, waiting for transfers between devices, reduce_terms(): return lax.psum(parts, 'col')  462 us
    psum x1, waiting for transfers between devices, local(): lax.psum(jnp.einsum('jr,js->rs', masked, masked, preferred_element_type=j...  187 us
    all_gather x1, waiting for transfers between devices, local(): tiles = lax.all_gather(item_factors, 'row', axis=1, tiled=True)  84.8 us
  transfers between devices with their start and end apart: 6, of which 6 were waited for; matrix products, arithmetic and copies ran while one was open for 2% of the time, Pallas kernels for 0%

commit v1 on v0

v1 whole, which is shorter than its diff:
```python
import functools
import heapq

import jax
import jax.numpy as jnp
from jax import lax
from jax.experimental import pallas as pl
from jax.experimental.pallas import tpu as pltpu
from jax.sharding import PartitionSpec as P

R = 256
HALF = 128
OBS = 2
ITERS = 3
TILES_COL = 4
UNITS = 2 * TILES_COL
RIDGE = 0.1
NX, NY, NZ = 4, 8, 8
A_UNITS = 5
MESH = pl.DeviceIdType.MESH


def plan(rows):
    a_us, b_us = 1.76 * rows / 64, 1.06 * rows / 64
    free = {}
    heap = []
    events = []
    order = []
    tick = [0]

    def send(now, piece):
        kind, axis, sign, hops, dx, dy, lo, hi = piece
        link = (axis, sign)
        start = max(now, free.get(link, 0.0))
        cost = (a_us if kind == "A" else b_us) * (hi - lo) / rows
        free[link] = start + cost
        tick[0] += 1
        heapq.heappush(heap, (start + cost + 1.6, tick[0], piece))
        order.append(piece)

    def spread(now, kind, axis, dx, dy, lo, hi):
        for sign in (1, -1):
            send(now, (kind, axis, sign, 1, dx, dy, lo, hi))

    spread(0.0, "A", "y", 0, 0, 0, rows)
    spread(0.0, "B", "x", 0, 0, 0, rows)
    spread(0.0, "A", "x", 0, 0, 0, rows)
    spread(0.0, "B", "y", 0, 0, 0, rows)
    events.append((None, list(order), 0.0))
    while heap:
        now, _, piece = heapq.heappop(heap)
        order.clear()
        kind, axis, sign, hops, dx, dy, lo, hi = piece
        ring = NX if axis == "x" else NY
        if axis == "x":
            dx = dx + sign
        else:
            dy = dy + sign
        if hops < ring // 2:
            middle = (lo + hi) // 2
            if hops < ring // 2 - 1:
                send(now, (kind, axis, sign, hops + 1, dx, dy, lo, hi))
            elif sign == 1:
                send(now, (kind, axis, sign, hops + 1, dx, dy, lo, middle))
            else:
                send(now, (kind, axis, sign, hops + 1, dx, dy, middle, hi))
        if kind == "A" and axis == "y":
            spread(now, "A", "x", dx, dy, lo, hi)
        if kind == "B" and axis == "x":
            spread(now, "B", "y", dx, dy, lo, hi)
        events.append((piece, list(order), now))
    return events


def kernel(
    counts,
    observed,
    conf_in,
    prev_in,
    words_in,
    item_hbm,
    out_ref,
    buf,
    picked,
    cs,
    seen,
    part,
    heard,
    vectors,
    gram,
    load_sem,
    send_sem,
    recv_sem,
    sum_send,
    sum_recv,
    vec_send,
    vec_recv,
    *,
    events,
    rows,
):
    me_row = lax.axis_index("row")
    me_col = lax.axis_index("col")
    my_x, my_y = me_row // NY, me_row % NY
    my_z, my_core = me_col // 2, me_col % 2
    span = NY * rows
    users = prev_in.shape[0]
    cols = 2 * NZ
    own = users // cols

    def at_row(dx, dy):
        return ((my_x + dx + NX) % NX) * NY + (my_y + dy + NY) % NY

    def base_row(row):
        return pl.multiple_of(row * rows, rows)

    peers = []
    for dz in sorted(range(NZ), key=lambda d: -min(d, NZ - d)):
        for flip in (0, 1):
            if dz or flip:
                peers.append(((my_z + dz) % NZ) * 2 + (my_core + flip) % 2)

    mine = base_row(me_row)
    loads = []
    for h in range(2):
        loads.append(
            pltpu.make_async_copy(
                item_hbm.at[:, :, pl.ds(h * HALF, HALF)],
                buf.at[pl.ds(h * TILES_COL, TILES_COL), pl.ds(mine, rows), :],
                load_sem.at[h],
            )
        )
        loads[-1].start()

    barrier = pltpu.get_barrier_semaphore()
    near = [at_row(1, 0), at_row(-1, 0), at_row(0, 1), at_row(0, -1)]
    for row in near:
        pl.semaphore_signal(barrier, inc=1, device_id=(row, me_col), device_id_type=MESH)
    for col in peers:
        pl.semaphore_signal(barrier, inc=1, device_id=(me_row, col), device_id_type=MESH)
    pl.semaphore_wait(barrier, len(near) + len(peers))
    for load in loads:
        load.wait()

    copies = {}

    def copy_of(piece):
        if piece not in copies:
            kind, axis, sign, hops, dx, dy, lo, hi = piece
            units = pl.ds(0, A_UNITS) if kind == "A" else pl.ds(A_UNITS, UNITS - A_UNITS)
            source = base_row(at_row(-dx, -dy))
            place = buf.at[units, pl.ds(source + lo, hi - lo), :]
            target = at_row(sign, 0) if axis == "x" else at_row(0, sign)
            index = len(copies)
            copies[piece] = pltpu.make_async_remote_copy(
                src_ref=place,
                dst_ref=place,
                send_sem=send_sem.at[index],
                recv_sem=recv_sem.at[index],
                device_id=(target, me_col),
                device_id_type=MESH,
            )
        return copies[piece]

    def expand():
        eye = lax.broadcasted_iota(jnp.int32, (users, users), 0) == lax.broadcasted_iota(
            jnp.int32, (users, users), 1
        )
        conf = jnp.sum(jnp.where(eye, conf_in[...], 0.0), axis=1, keepdims=True)
        words_wide = words_in.shape[1]
        lanes = 8 * words_wide
        word_of = lax.broadcasted_iota(jnp.int32, (words_wide, lanes), 0)
        slot_of = lax.broadcasted_iota(jnp.int32, (words_wide, lanes), 1)
        scale = 1.0 / jnp.left_shift(1, slot_of & 7).astype(jnp.float32)
        spreader = jnp.where((slot_of >> 3) == word_of, scale, 0.0).astype(jnp.bfloat16)
        for s in range(OBS):
            count = counts[observed[0, s]]
            for half in range(words_in.shape[0] // (users * OBS)):
                words = words_in[pl.ds(half * OBS + s, users, stride=words_in.shape[0] // users), :]
                shifted = jnp.dot(
                    words.astype(jnp.float32).astype(jnp.bfloat16),
                    spreader,
                    preferred_element_type=jnp.float32,
                ).astype(jnp.int32)
                slot = half * lanes + lax.broadcasted_iota(jnp.int32, (users, lanes), 1)
                on = jnp.where(slot < count, shifted & 1, 0).astype(jnp.float32)
                for piece in range(lanes // span):
                    chunk = half * (lanes // span) + piece
                    here = on[:, piece * span : (piece + 1) * span]
                    seen[s, chunk] = here.astype(jnp.bfloat16)
                    cs[s, chunk] = conf * here
        return conf

    def rows_of(tile, chunk):
        place = pl.ds(pl.multiple_of(chunk * span, span), span)
        return jnp.concatenate([buf[tile, place, :], buf[TILES_COL + tile, place, :]], axis=1)

    def weighted(rounded, s, chunk):
        items = picked[s, chunk]
        scores = lax.dot_general(
            rounded, items, (((1,), (1,)), ((), ())), preferred_element_type=jnp.float32
        )
        weights = (cs[s, chunk] * scores).astype(jnp.bfloat16)
        return jnp.dot(weights, items, preferred_element_type=jnp.float32)

    for piece in events[0][1]:
        copy_of(piece).start()
    start = prev_in[...].astype(jnp.float32)
    vectors[0] = start
    gram[...] = jnp.zeros_like(gram)
    part[0] = jnp.zeros_like(start)
    conf = expand()

    def first_pass(chunk):
        slot = chunk * span + lax.broadcasted_iota(jnp.int32, (span, R), 0)
        choice = [None] * OBS
        total = gram[...]
        for tile in range(TILES_COL):
            items = rows_of(tile, chunk)
            for s in range(OBS):
                choice[s] = (
                    items if tile == 0 else jnp.where(observed[0, s] == tile, items, choice[s])
                )
            valid = jnp.where(slot < counts[tile], 1.0, 0.0).astype(jnp.bfloat16)
            total = total + lax.dot_general(
                valid * items, items, (((0,), (0,)), ((), ())), preferred_element_type=jnp.float32
            )
        gram[...] = total
        sums = part[0]
        for s in range(OBS):
            picked[s, chunk] = choice[s]
            sums = sums + (1.0 + conf) * jnp.dot(
                seen[s, chunk], choice[s], preferred_element_type=jnp.float32
            )
            sums = sums - weighted(prev_in[...], s, chunk)
        part[0] = sums

    for piece, follow, _ in events[1:]:
        copy_of(piece).wait_recv()
        for other in follow:
            copy_of(other).start()

    for dx in (0, 1, 3, 2):
        first_pass((my_x + dx) % NX)

    mine_users = pl.ds(pl.multiple_of(me_col * own, own), own)
    waits = []

    def with_gram(vector):
        return jnp.dot(vector, gram[...], precision=lax.Precision.HIGHEST)

    def exchange_sums(k):
        for col in peers:
            copy = pltpu.make_async_remote_copy(
                src_ref=part.at[k, pl.ds(pl.multiple_of(col * own, own), own), :],
                dst_ref=heard.at[k, me_col],
                send_sem=sum_send.at[k],
                recv_sem=sum_recv.at[k],
                device_id=(me_row, col),
                device_id_type=MESH,
            )
            copy.start()
        heard[k, me_col] = part[k, mine_users, :]
        several = heard.at[k, pl.ds(0, cols - 1)]
        pltpu.make_async_copy(several, several, sum_recv.at[k]).wait()
        waits.append((several, sum_send.at[k]))
        total = heard[k, 0]
        for col in range(1, cols):
            total = total + heard[k, col]
        return total

    def share(k, value):
        vectors[k, mine_users, :] = value
        for col in peers:
            copy = pltpu.make_async_remote_copy(
                src_ref=vectors.at[k, mine_users, :],
                dst_ref=vectors.at[k, mine_users, :],
                send_sem=vec_send.at[k],
                recv_sem=vec_recv.at[k],
                device_id=(me_row, col),
                device_id_type=MESH,
            )
            copy.start()
        several = vectors.at[k, pl.ds(0, own * (cols - 1)), :]
        pltpu.make_async_copy(several, several, vec_recv.at[k]).wait()
        waits.append((several, vec_send.at[k]))

    part[0] = part[0] - with_gram(start)
    answer = vectors[0, mine_users, :]
    residual = exchange_sums(0) - RIDGE * answer
    direction = residual
    norm_now = jnp.sum(residual * residual, axis=1, keepdims=True)
    for k in range(1, ITERS + 1):
        share(k, direction)
        vector = vectors[k]
        rounded = vector.astype(jnp.bfloat16)
        sums = with_gram(vector)
        for s in range(OBS):
            for chunk in range(NX):
                sums = sums + weighted(rounded, s, chunk)
        part[k] = sums
        image = exchange_sums(k) + RIDGE * direction
        step_size = norm_now / jnp.sum(direction * image, axis=1, keepdims=True)
        answer = answer + step_size * direction
        if k < ITERS:
            residual = residual - step_size * image
            norm_next = jnp.sum(residual * residual, axis=1, keepdims=True)
            direction = residual + (norm_next / norm_now) * direction
            norm_now = norm_next
    share(ITERS + 1, answer)
    out_ref[...] = vectors[ITERS + 1]

    for piece in copies:
        copies[piece].wait_send()
    for several, sem in waits:
        pltpu.make_async_copy(several, several, sem).wait()


def local(item_factors, tile_counts, observed_tiles, mask_words, confidence, previous):
    rows = item_factors.shape[1]
    users, slots, words = mask_words.shape
    tile_len = NX * NY * rows
    events = plan(rows)
    messages = sum(len(follow) for _, follow, _ in events)
    flat = (
        mask_words.reshape(users, slots, words // HALF, HALF)
        .transpose(0, 2, 1, 3)
        .reshape(users * slots * (words // HALF), HALF)
    )
    vmem = pl.BlockSpec(memory_space=pltpu.VMEM)
    smem = pl.BlockSpec(memory_space=pltpu.SMEM)
    cols = 2 * NZ
    return pl.pallas_call(
        functools.partial(kernel, events=events, rows=rows),
        out_shape=jax.ShapeDtypeStruct((users, R), jnp.float32),
        in_specs=[smem, smem, vmem, vmem, vmem, pl.BlockSpec(memory_space=pl.ANY)],
        out_specs=vmem,
        scratch_shapes=[
            pltpu.VMEM((UNITS, tile_len, HALF), jnp.bfloat16),
            pltpu.VMEM((OBS, NX, NY * rows, R), jnp.bfloat16),
            pltpu.VMEM((OBS, NX, users, NY * rows), jnp.float32),
            pltpu.VMEM((OBS, NX, users, NY * rows), jnp.bfloat16),
            pltpu.VMEM((ITERS + 1, users, R), jnp.float32),
            pltpu.VMEM((ITERS + 1, cols, users // cols, R), jnp.float32),
            pltpu.VMEM((ITERS + 2, users, R), jnp.float32),
            pltpu.VMEM((R, R), jnp.float32),
            pltpu.SemaphoreType.DMA((2,)),
            pltpu.SemaphoreType.DMA((messages,)),
            pltpu.SemaphoreType.DMA((messages,)),
            pltpu.SemaphoreType.DMA((ITERS + 1,)),
            pltpu.SemaphoreType.DMA((ITERS + 1,)),
            pltpu.SemaphoreType.DMA((ITERS + 2,)),
            pltpu.SemaphoreType.DMA((ITERS + 2,)),
        ],
        compiler_params=pltpu.CompilerParams(
            collective_id=0, has_side_effects=True, vmem_limit_bytes=48 * 2**20
        ),
    )(tile_counts, observed_tiles, confidence.reshape(1, users), previous, flat, item_factors)


def solution(mesh):
    return jax.shard_map(
        local,
        mesh=mesh,
        in_specs=(
            P("col", "row", None),
            P("col"),
            P("row", "col"),
            P("row", "col", None),
            P("row"),
            P("row", None),
        ),
        out_specs=P("row", None),
        check_vma=False,
    )
```

time: 784 us -> 104 us (0.13)
  waiting for transfers between devices: 735 us -> 0 us
  Pallas kernels: 0 us -> 99.6 us
  matrix products: 23.4 us -> 0 us
  between operations: 15.3 us -> 0.02 us
    psum x5 -> x0, waiting for transfers between devices: 649 us -> none  [the longest x4 462 us: reduce_terms(): return lax.psum(parts, 'col')]
    pallas_call x0 -> x1, Pallas kernels: none -> 99.6 us  [local(): pl.pallas_call(functools.partial(kernel, events=events, rows=rows), out_s...]
    all_gather x1 -> x0, waiting for transfers between devices: 84.8 us -> none  [local(): tiles = lax.all_gather(item_factors, 'row', axis=1, tiled=True)]
    dot_general x15 -> x0, matrix products: 23.4 us -> none  [the longest x8 14.9 us: weighted(): jnp.dot(weights, slot_tiles[slot], preferred_element_type=jnp.float32)]
  transfers between devices with their start and end apart: 6 -> 0, of which waited for: 6 -> 0; matrix products, arithmetic and copies ran while one was open for 2% -> 0% of each run, Pallas kernels for 0% -> 0%
where the time goes in v1:
time: 104 us
  Pallas kernels  99.6 us (96%)
  local copies, waits for them, and re-layouts  4.03 us (4%)
    pallas_call x1, Pallas kernels, local(): pl.pallas_call(functools.partial(kernel, events=events, rows=rows), out_s...  99.6 us
    unnamed x13, local copies, waits for them, and re-layouts  4.03 us

profile of v1, /device:TPU:1, one launch (start us, length us, event | category | flops | bytes accessed | tf_op | source)
XLA Modules:
  0.0 103.6 jit_solution(16664534870602716079)
XLA Ops:
  0.0 0.0 copy-start.3
  0.0 0.0 copy-start.4
  0.0 0.0 copy-start.5
  0.0 0.6 copy-done.3
  0.7 0.0 copy-done.4
  0.7 0.0 copy-done.5
  0.7 0.0 copy-start
  0.7 0.9 copy-done
  1.6 0.0 copy-start.1
  1.6 0.9 copy-done.1
  2.5 0.0 copy-start.2
  2.5 0.8 copy-done.2
  3.4 99.6 %shard_map.64 = f32[128,256]{1,0:T(8,128)S(1)} custom-call(s32[4]{0:T(128)S(1)} %copy-done.3, s32[1,2]{1,0:T(1,128)S(1)} %copy-done.4, f32[1,128]{1,0:T(1,128)S(1)} %bitcast.7, bf16[128,256]{1,0:T(8,128)(2,1)S(1)} %copy-done.2, s32[512,128]{1,0:T(8,128)S(1)} %bitcast.6, bf16[4,64,256]{2,1,0:T(8,128)(2,1)S(1)} %copy-done.1), custom_call_target="tpu_custom_call" | custom-call | tf_op jit(solution)/shard_map/pallas_call | solution.py:333
  103.0 0.7 copy.9
Async XLA Ops:
  0.0 0.7 copy-start.3
  0.0 0.7 copy-start.4
  0.0 0.7 copy-start.5
  0.7 0.9 copy-start
  1.6 0.9 copy-start.1
  2.5 0.8 copy-start.2

commit v2 on v1

v2 whole, which is shorter than its diff:
```python
import functools
import heapq
import itertools

import jax
import jax.numpy as jnp
from jax import lax
from jax.experimental import pallas as pl
from jax.experimental.pallas import tpu as pltpu
from jax.sharding import PartitionSpec as P

R = 256
HALF = 128
OBS = 2
ITERS = 3
TILES_COL = 4
UNITS = 2 * TILES_COL
RIDGE = 0.1
NX, NY, NZ = 4, 8, 8
A_UNITS = 5
MESH = pl.DeviceIdType.MESH


def plan(rows):
    a_us, b_us = 1.76 * A_UNITS / 5, 1.76 * (UNITS - A_UNITS) / 5
    free = {}
    heap = []
    order = []
    ready = []
    events = []
    tick = itertools.count()

    def queue(*piece):
        kind, axis, _, hops = piece[:4]
        if kind == "A":
            left = 6 - hops if axis == "y" else 2 - hops
        else:
            left = 6 - hops if axis == "x" else 4 - hops
        ready.append((-left, next(tick), piece))

    def flush(now):
        for _, _, piece in sorted(ready):
            kind, axis, sign, lo, hi, stride = piece[0], piece[1], piece[2], *piece[6:]
            cost = (a_us if kind == "A" else b_us) * (hi - lo) / rows
            begin = max(now, free.get((axis, sign), 0.0))
            free[axis, sign] = begin + cost * stride
            heapq.heappush(heap, (begin + cost + 2.5 + 0.5 * stride, next(tick), piece))
            order.append(piece)
        ready.clear()
        events.append((heard[0], list(order), now))
        order.clear()

    def spread(kind, axis, dx, dy, lo, hi):
        for stride in (2, 1) if (kind, axis) == ("A", "y") else (1,):
            for sign in (1, -1):
                queue(kind, axis, sign, stride, dx, dy, lo, hi, stride)

    heard = [None]
    spread("A", "y", 0, 0, 0, rows)
    spread("B", "x", 0, 0, 0, rows)
    spread("A", "x", 0, 0, 0, rows)
    spread("B", "y", 0, 0, 0, rows)
    flush(0.0)
    while heap:
        now, _, heard[0] = heapq.heappop(heap)
        kind, axis, sign, hops, dx, dy, lo, hi, stride = heard[0]
        last = (NX if axis == "x" else NY) // 2
        if axis == "x":
            dx += sign * stride
        else:
            dy += sign * stride
        if hops < last and not (kind == "A" and axis == "y" and hops == 1):
            middle = (lo + hi) // 2
            if hops < last - 1:
                queue(kind, axis, sign, hops + 1, dx, dy, lo, hi, 1)
            elif sign == 1:
                queue(kind, axis, sign, hops + 1, dx, dy, lo, middle, 1)
            else:
                queue(kind, axis, sign, hops + 1, dx, dy, middle, hi, 1)
        if (kind, axis) == ("A", "y"):
            spread("A", "x", dx, dy, lo, hi)
        if (kind, axis) == ("B", "x"):
            spread("B", "y", dx, dy, lo, hi)
        flush(now)
    return events


def kernel(
    counts_hbm,
    observed_hbm,
    conf_hbm,
    prev_hbm,
    words_hbm,
    item_hbm,
    out_ref,
    buf,
    picked,
    cs,
    seen,
    part,
    heard,
    high,
    low,
    steps,
    dots,
    gram,
    counts,
    observed,
    conf_in,
    prev_in,
    words_in,
    load_sem,
    send_sem,
    recv_sem,
    sum_send,
    sum_recv,
    high_send,
    high_recv,
    low_send,
    low_recv,
    step_sem,
    dot_sem,
    *,
    events,
    rows,
):
    me_row = lax.axis_index("row")
    me_col = lax.axis_index("col")
    my_x, my_y = me_row // NY, me_row % NY
    my_z, my_core = me_col // 2, me_col % 2
    span = NY * rows
    users = prev_in.shape[0]
    cols = 2 * NZ
    own = users // cols

    def at_row(dx, dy):
        return ((my_x + dx + NX) % NX) * NY + (my_y + dy + NY) % NY

    def base_row(row):
        return pl.multiple_of(row * rows, rows)

    peers = []
    for dz in sorted(range(NZ), key=lambda d: -min(d, NZ - d)):
        for flip in (0, 1):
            if dz or flip:
                peers.append(((my_z + dz) % NZ) * 2 + (my_core + flip) % 2)

    mine = base_row(me_row)
    loads = []
    for h in range(2):
        loads.append(
            pltpu.make_async_copy(
                item_hbm.at[:, :, pl.ds(h * HALF, HALF)],
                buf.at[pl.ds(h * TILES_COL, TILES_COL), pl.ds(mine, rows), :],
                load_sem.at[h],
            )
        )
        loads[-1].start()
    others = []
    for i, (src, dst) in enumerate(
        (
            (words_hbm, words_in),
            (counts_hbm, counts),
            (observed_hbm, observed),
            (conf_hbm, conf_in),
            (prev_hbm, prev_in),
        )
    ):
        others.append(pltpu.make_async_copy(src, dst, load_sem.at[2 + i]))
        others[-1].start()

    barrier = pltpu.get_barrier_semaphore()
    near = [at_row(1, 0), at_row(-1, 0)] + [at_row(0, d) for d in (1, -1, 2, -2)]
    for row in near:
        pl.semaphore_signal(barrier, inc=1, device_id=(row, me_col), device_id_type=MESH)
    for col in peers:
        pl.semaphore_signal(barrier, inc=1, device_id=(me_row, col), device_id_type=MESH)
    pl.semaphore_wait(barrier, len(near) + len(peers))
    for load in loads:
        load.wait()

    copies = {}

    def copy_of(piece):
        if piece not in copies:
            kind, axis, sign, _, dx, dy, lo, hi, stride = piece
            units = pl.ds(0, A_UNITS) if kind == "A" else pl.ds(A_UNITS, UNITS - A_UNITS)
            source = base_row(at_row(-dx, -dy))
            place = buf.at[units, pl.ds(source + lo, hi - lo), :]
            target = at_row(sign, 0) if axis == "x" else at_row(0, sign * stride)
            index = len(copies)
            copies[piece] = pltpu.make_async_remote_copy(
                src_ref=place,
                dst_ref=place,
                send_sem=send_sem.at[index],
                recv_sem=recv_sem.at[index],
                device_id=(target, me_col),
                device_id_type=MESH,
            )
        return copies[piece]

    eye = lax.broadcasted_iota(jnp.int32, (users, users), 0) == lax.broadcasted_iota(
        jnp.int32, (users, users), 1
    )

    def column(row):
        return jnp.sum(jnp.where(eye, row, 0.0), axis=1, keepdims=True)

    def expand():
        conf = column(conf_in[...])
        words_wide = words_in.shape[1]
        lanes = 8 * words_wide
        word_of = lax.broadcasted_iota(jnp.int32, (words_wide, lanes), 0)
        slot_of = lax.broadcasted_iota(jnp.int32, (words_wide, lanes), 1)
        scale = 1.0 / jnp.left_shift(1, slot_of & 7).astype(jnp.float32)
        spreader = jnp.where((slot_of >> 3) == word_of, scale, 0.0).astype(jnp.bfloat16)
        for s in range(OBS):
            count = counts[observed[0, s]]
            for half in range(words_in.shape[0] // (users * OBS)):
                words = words_in[pl.ds(half * OBS + s, users, stride=words_in.shape[0] // users), :]
                shifted = jnp.dot(
                    words.astype(jnp.float32).astype(jnp.bfloat16),
                    spreader,
                    preferred_element_type=jnp.float32,
                ).astype(jnp.int32)
                slot = half * lanes + lax.broadcasted_iota(jnp.int32, (users, lanes), 1)
                on = jnp.where(slot < count, shifted & 1, 0).astype(jnp.float32)
                for piece in range(lanes // span):
                    chunk = half * (lanes // span) + piece
                    here = on[:, piece * span : (piece + 1) * span]
                    seen[s, chunk] = here.astype(jnp.bfloat16)
                    cs[s, chunk] = conf * here
        return conf

    def rows_of(tile, chunk):
        place = pl.ds(pl.multiple_of(chunk * span, span), span)
        return jnp.concatenate([buf[tile, place, :], buf[TILES_COL + tile, place, :]], axis=1)

    def weighted(rounded, s, chunk):
        items = picked[s, chunk]
        scores = lax.dot_general(
            rounded, items, (((1,), (1,)), ((), ())), preferred_element_type=jnp.float32
        )
        weights = (cs[s, chunk] * scores).astype(jnp.bfloat16)
        return jnp.dot(weights, items, preferred_element_type=jnp.float32)

    for piece in events[0][1]:
        copy_of(piece).start()
    for load in others:
        load.wait()
    gram[...] = jnp.zeros_like(gram)
    part[0] = jnp.zeros((users, R), jnp.float32)
    conf = expand()

    def first_pass(chunk):
        slot = chunk * span + lax.broadcasted_iota(jnp.int32, (span, R), 0)
        choice = [None] * OBS
        total = gram[...]
        for tile in range(TILES_COL):
            items = rows_of(tile, chunk)
            for s in range(OBS):
                choice[s] = (
                    items if tile == 0 else jnp.where(observed[0, s] == tile, items, choice[s])
                )
            valid = jnp.where(slot < counts[tile], 1.0, 0.0).astype(jnp.bfloat16)
            total = total + lax.dot_general(
                valid * items, items, (((0,), (0,)), ((), ())), preferred_element_type=jnp.float32
            )
        gram[...] = total
        sums = part[0]
        for s in range(OBS):
            picked[s, chunk] = choice[s]
            sums = sums + (1.0 + conf) * jnp.dot(
                seen[s, chunk], choice[s], preferred_element_type=jnp.float32
            )
            sums = sums - weighted(prev_in[...], s, chunk)
        part[0] = sums

    done = {}
    for index, (piece, _, _) in enumerate(events[1:]):
        _, axis, sign, _, dx, _, _, _, stride = piece
        done[(-dx - (sign * stride if axis == "x" else 0)) % NX] = index
    for index, (piece, follow, _) in enumerate(events[1:]):
        copy_of(piece).wait_recv()
        for other in follow:
            copy_of(other).start()
        for dx in range(NX):
            if done[dx] == index:
                first_pass((my_x + dx) % NX)

    waits = []

    def finish(ref, sem):
        pltpu.make_async_copy(ref, ref, sem).wait()

    def to_peers(place, send, recv):
        for col in peers:
            pltpu.make_async_remote_copy(
                src_ref=place.at[me_col],
                dst_ref=place.at[me_col],
                send_sem=send,
                recv_sem=recv,
                device_id=(me_row, col),
                device_id_type=MESH,
            ).start()
        waits.append((place.at[pl.ds(0, cols - 1)], send))

    def with_gram(vector):
        return jnp.dot(
            vector,
            gram[...],
            precision=lax.Precision.HIGHEST,
            preferred_element_type=jnp.float32,
        )

    def exchange_sums(k):
        for col in peers:
            pltpu.make_async_remote_copy(
                src_ref=part.at[k, pl.ds(pl.multiple_of(col * own, own), own), :],
                dst_ref=heard.at[k, me_col],
                send_sem=sum_send.at[k],
                recv_sem=sum_recv.at[k],
                device_id=(me_row, col),
                device_id_type=MESH,
            ).start()
        heard[k, me_col] = part[k, pl.ds(pl.multiple_of(me_col * own, own), own), :]
        several = heard.at[k, pl.ds(0, cols - 1)]
        waits.append((several, sum_send.at[k]))
        finish(several, sum_recv.at[k])
        total = heard[k, 0]
        for col in range(1, cols):
            total = total + heard[k, col]
        return total

    def whole(ref, k):
        return ref[k].astype(jnp.float32).reshape(users, R)

    start = prev_in[...].astype(jnp.float32)
    part[0] = part[0] - with_gram(start)
    mine_users = (
        lax.broadcasted_iota(jnp.int32, (own, users), 1)
        == me_col * own + lax.broadcasted_iota(jnp.int32, (own, users), 0)
    ).astype(jnp.float32).astype(jnp.bfloat16)
    ours = jnp.dot(mine_users, prev_in[...], preferred_element_type=jnp.float32)
    residual = exchange_sums(0) - RIDGE * ours
    direction = residual
    norm_now = jnp.sum(residual * residual, axis=1, keepdims=True)
    lane = lax.broadcasted_iota(jnp.int32, (own, HALF), 1)
    scalars = jnp.zeros((own, HALF), jnp.float32)
    for k in range(ITERS):
        top = direction.astype(jnp.bfloat16)
        rest = (direction - top.astype(jnp.float32)).astype(jnp.bfloat16)
        high[k, me_col] = top
        low[k, me_col] = rest
        to_peers(high.at[k], high_send.at[k], high_recv.at[k])
        to_peers(low.at[k], low_send.at[k], low_recv.at[k])
        if k == ITERS - 1:
            steps[me_col] = jnp.where(lane == k, norm_now, scalars)
            to_peers(steps, step_sem.at[0], step_sem.at[1])
        direction = top.astype(jnp.float32) + rest.astype(jnp.float32)
        finish(high.at[k, pl.ds(0, cols - 1)], high_recv.at[k])
        upper = whole(high, k)
        rounded = upper.astype(jnp.bfloat16)
        sums = jnp.zeros((users, R), jnp.float32)
        for s in range(OBS):
            for chunk in range(NX):
                sums = sums + weighted(rounded, s, chunk)
        finish(low.at[k, pl.ds(0, cols - 1)], low_recv.at[k])
        vector = upper + whole(low, k)
        sums = sums + with_gram(vector)
        if k == ITERS - 1:
            break
        part[k + 1] = sums
        image = exchange_sums(k + 1) + RIDGE * direction
        step_size = norm_now / jnp.sum(direction * image, axis=1, keepdims=True)
        scalars = jnp.where(lane == k, step_size, scalars)
        residual = residual - step_size * image
        norm_next = jnp.sum(residual * residual, axis=1, keepdims=True)
        direction = residual + (norm_next / norm_now) * direction
        norm_now = norm_next

    dot_here = jnp.sum(sums * vector, axis=1, keepdims=True)
    dots[me_col] = jnp.broadcast_to(
        jnp.sum(jnp.where(eye, dot_here, 0.0), axis=0, keepdims=True), (8, users)
    )
    to_peers(dots, dot_sem.at[0], dot_sem.at[1])
    finish(steps.at[pl.ds(0, cols - 1)], step_sem.at[1])
    known = steps[...].reshape(users, HALF)
    answer = start
    for k in range(ITERS - 1):
        answer = answer + known[:, k : k + 1] * (whole(high, k) + whole(low, k))
    ridge = RIDGE * jnp.sum(vector * vector, axis=1, keepdims=True)
    finish(dots.at[pl.ds(0, cols - 1)], dot_sem.at[1])
    total = dots[0, 0:1]
    for col in range(1, cols):
        total = total + dots[col, 0:1]
    step_size = known[:, ITERS - 1 : ITERS] / (column(total) + ridge)
    out_ref[...] = answer + step_size * vector

    for piece in copies:
        copies[piece].wait_send()
    for several, sem in waits:
        finish(several, sem)


def local(item_factors, tile_counts, observed_tiles, mask_words, confidence, previous):
    rows = item_factors.shape[1]
    users, slots, words = mask_words.shape
    tile_len = NX * NY * rows
    events = plan(rows)
    messages = sum(len(follow) for _, follow, _ in events)
    flat = (
        mask_words.reshape(users, slots, words // HALF, HALF)
        .transpose(0, 2, 1, 3)
        .reshape(users * slots * (words // HALF), HALF)
    )
    anywhere = pl.BlockSpec(memory_space=pl.ANY)
    cols = 2 * NZ
    own = users // cols
    sems = pltpu.SemaphoreType.DMA
    return pl.pallas_call(
        functools.partial(kernel, events=events, rows=rows),
        out_shape=jax.ShapeDtypeStruct((users, R), jnp.float32),
        in_specs=[anywhere] * 6,
        out_specs=pl.BlockSpec(memory_space=pltpu.VMEM),
        scratch_shapes=[
            pltpu.VMEM((UNITS, tile_len, HALF), jnp.bfloat16),
            pltpu.VMEM((OBS, NX, NY * rows, R), jnp.bfloat16),
            pltpu.VMEM((OBS, NX, users, NY * rows), jnp.float32),
            pltpu.VMEM((OBS, NX, users, NY * rows), jnp.bfloat16),
            pltpu.VMEM((ITERS, users, R), jnp.float32),
            pltpu.VMEM((ITERS, cols, own, R), jnp.float32),
            pltpu.VMEM((ITERS, cols, own, R), jnp.bfloat16),
            pltpu.VMEM((ITERS, cols, own, R), jnp.bfloat16),
            pltpu.VMEM((cols, own, HALF), jnp.float32),
            pltpu.VMEM((cols, 8, users), jnp.float32),
            pltpu.VMEM((R, R), jnp.float32),
            pltpu.SMEM(tile_counts.shape, jnp.int32),
            pltpu.SMEM(observed_tiles.shape, jnp.int32),
            pltpu.VMEM((1, users), jnp.float32),
            pltpu.VMEM((users, R), jnp.bfloat16),
            pltpu.VMEM(flat.shape, jnp.int32),
            sems((7,)),
            sems((messages,)),
            sems((messages,)),
        ]
        + [sems((ITERS,))] * 6
        + [sems((2,))] * 2,
        compiler_params=pltpu.CompilerParams(
            collective_id=0, has_side_effects=True, vmem_limit_bytes=60 * 1024 * 1024
        ),
    )(tile_counts, observed_tiles, confidence.reshape(1, users), previous, flat, item_factors)


def solution(mesh):
    return jax.shard_map(
        local,
        mesh=mesh,
        in_specs=(
            P("col", "row", None),
            P("col"),
            P("row", "col"),
            P("row", "col", None),
            P("row"),
            P("row", None),
        ),
        out_specs=P("row", None),
        check_vma=False,
    )
```

time: 104 us -> 90.6 us (0.87)
  Pallas kernels: 99.6 us -> 88.9 us
  local copies, waits for them, and re-layouts: 4.03 us -> 1.57 us
    pallas_call x1, Pallas kernels: 99.6 us -> 88.9 us  [local(): pl.pallas_call(functools.partial(kernel, events=events, rows=rows), out_s...]
    unnamed x13 -> x1, local copies, waits for them, and re-layouts: 4.03 us -> 1.57 us
where the time goes in v2:
time: 90.6 us; the launch traced here: 90.4 us
  Pallas kernels  88.9 us (98%)
  local copies, waits for them, and re-layouts  1.57 us (2%)
    pallas_call x1, Pallas kernels, local(): pl.pallas_call(functools.partial(kernel, events=events, rows=rows), out_s...  88.9 us

profile of v2, /device:TPU:1, one launch (start us, length us, event | category | flops | bytes accessed | tf_op | source)
XLA Modules:
  0.0 90.4 jit_solution(18061216190261529083)
XLA Ops:
  0.0 88.9 %shard_map.64 = f32[128,256]{1,0:T(8,128)} custom-call(s32[4]{0:T(128)} %counts_hbm.1, s32[1,2]{1,0:T(1,128)} %observed_hbm.1, f32[1,128]{1,0:T(1,128)} %bitcast.7, bf16[128,256]{1,0:T(8,128)(2,1)} %prev_hbm.1, s32[512,128]{1,0:T(8,128)} %bitcast.6, bf16[4,64,256]{2,1,0:T(8,128)(2,1)} %item_hbm.1), custom_call_target="tpu_custom_call" | custom-call | tf_op jit(solution)/shard_map/pallas_call | solution.py:421
  88.9 1.6 %copy.9 = f32[128,256]{1,0:T(8,128)} copy(f32[128,256]{1,0:T(8,128)} %shard_map.64) | data formatting | bytes 262144

commit v3 on v2

--- a/solution.py
+++ b/solution.py
@@ -21,49 +21,49 @@
 MESH = pl.DeviceIdType.MESH
 
 
+SPLIT = 1
+
+
 def plan(rows):
-    a_us, b_us = 1.76 * A_UNITS / 5, 1.76 * (UNITS - A_UNITS) / 5
-    free = {}
+    unit_us = 1.76 / 5
+    costs = {"A": unit_us * A_UNITS, "B": unit_us * (UNITS - A_UNITS)}
+    free = {(axis, sign): 0.0 for axis in "xy" for sign in (1, -1)}
+    waiting = {link: [] for link in free}
     heap = []
-    order = []
-    ready = []
     events = []
     tick = itertools.count()
 
     def queue(*piece):
-        kind, axis, _, hops = piece[:4]
-        if kind == "A":
-            left = 6 - hops if axis == "y" else 2 - hops
-        else:
-            left = 6 - hops if axis == "x" else 4 - hops
-        ready.append((-left, next(tick), piece))
-
-    def flush(now):
-        for _, _, piece in sorted(ready):
-            kind, axis, sign, lo, hi, stride = piece[0], piece[1], piece[2], *piece[6:]
-            cost = (a_us if kind == "A" else b_us) * (hi - lo) / rows
-            begin = max(now, free.get((axis, sign), 0.0))
-            free[axis, sign] = begin + cost * stride
-            heapq.heappush(heap, (begin + cost + 2.5 + 0.5 * stride, next(tick), piece))
-            order.append(piece)
-        ready.clear()
-        events.append((heard[0], list(order), now))
-        order.clear()
+        kind, axis, sign, hops, dx, dy = piece[:6]
+        turn = -(6 - hops if (kind, axis) in (("A", "y"), ("B", "x")) else (2 if kind == "A" else 4) - hops)
+        heapq.heappush(waiting[axis, sign], (turn, next(tick), piece))
+
+    def flush(now, heard):
+        order = []
+        for link, line in waiting.items():
+            while line:
+                piece = heapq.heappop(line)[2]
+                lo, hi, stride = piece[6:]
+                cost = costs[piece[0]] * (hi - lo) / rows
+                begin = max(now, free[link])
+                free[link] = begin + cost * stride
+                heapq.heappush(heap, (begin + cost + 2.5 + 0.5 * stride, next(tick), piece))
+                order.append(piece)
+        events.append((heard, order, now))
 
     def spread(kind, axis, dx, dy, lo, hi):
         for stride in (2, 1) if (kind, axis) == ("A", "y") else (1,):
             for sign in (1, -1):
                 queue(kind, axis, sign, stride, dx, dy, lo, hi, stride)
 
-    heard = [None]
-    spread("A", "y", 0, 0, 0, rows)
-    spread("B", "x", 0, 0, 0, rows)
-    spread("A", "x", 0, 0, 0, rows)
-    spread("B", "y", 0, 0, 0, rows)
-    flush(0.0)
+    for part in range(SPLIT):
+        lo, hi = rows * part // SPLIT, rows * (part + 1) // SPLIT
+        for kind, axis in (("A", "y"), ("B", "x"), ("A", "x"), ("B", "y")):
+            spread(kind, axis, 0, 0, lo, hi)
+    flush(0.0, None)
     while heap:
-        now, _, heard[0] = heapq.heappop(heap)
-        kind, axis, sign, hops, dx, dy, lo, hi, stride = heard[0]
+        now, _, heard = heapq.heappop(heap)
+        kind, axis, sign, hops, dx, dy, lo, hi, stride = heard
         last = (NX if axis == "x" else NY) // 2
         if axis == "x":
             dx += sign * stride
@@ -81,7 +81,7 @@
             spread("A", "x", dx, dy, lo, hi)
         if (kind, axis) == ("B", "x"):
             spread("B", "y", dx, dy, lo, hi)
-        flush(now)
+        flush(now, heard)
     return events
 
 
@@ -95,6 +95,7 @@
     out_ref,
     buf,
     picked,
+    turned,
     cs,
     seen,
     part,
@@ -146,6 +147,12 @@
                 peers.append(((my_z + dz) % NZ) * 2 + (my_core + flip) % 2)
 
     mine = base_row(me_row)
+    barrier = pltpu.get_barrier_semaphore()
+    near = [at_row(1, 0), at_row(-1, 0)] + [at_row(0, d) for d in (1, -1, 2, -2)]
+    for row in near:
+        pl.semaphore_signal(barrier, inc=1, device_id=(row, me_col), device_id_type=MESH)
+    for col in peers:
+        pl.semaphore_signal(barrier, inc=1, device_id=(me_row, col), device_id_type=MESH)
     loads = []
     for h in range(2):
         loads.append(
@@ -169,12 +176,6 @@
         others.append(pltpu.make_async_copy(src, dst, load_sem.at[2 + i]))
         others[-1].start()
 
-    barrier = pltpu.get_barrier_semaphore()
-    near = [at_row(1, 0), at_row(-1, 0)] + [at_row(0, d) for d in (1, -1, 2, -2)]
-    for row in near:
-        pl.semaphore_signal(barrier, inc=1, device_id=(row, me_col), device_id_type=MESH)
-    for col in peers:
-        pl.semaphore_signal(barrier, inc=1, device_id=(me_row, col), device_id_type=MESH)
     pl.semaphore_wait(barrier, len(near) + len(peers))
     for load in loads:
         load.wait()
@@ -237,12 +238,9 @@
         return jnp.concatenate([buf[tile, place, :], buf[TILES_COL + tile, place, :]], axis=1)
 
     def weighted(rounded, s, chunk):
-        items = picked[s, chunk]
-        scores = lax.dot_general(
-            rounded, items, (((1,), (1,)), ((), ())), preferred_element_type=jnp.float32
-        )
+        scores = jnp.dot(rounded, turned[s, chunk], preferred_element_type=jnp.float32)
         weights = (cs[s, chunk] * scores).astype(jnp.bfloat16)
-        return jnp.dot(weights, items, preferred_element_type=jnp.float32)
+        return jnp.dot(weights, picked[s, chunk], preferred_element_type=jnp.float32)
 
     for piece in events[0][1]:
         copy_of(piece).start()
@@ -270,6 +268,7 @@
         sums = part[0]
         for s in range(OBS):
             picked[s, chunk] = choice[s]
+            turned[s, chunk] = choice[s].T
             sums = sums + (1.0 + conf) * jnp.dot(
                 seen[s, chunk], choice[s], preferred_element_type=jnp.float32
             )
@@ -414,7 +413,7 @@
         .transpose(0, 2, 1, 3)
         .reshape(users * slots * (words // HALF), HALF)
     )
-    anywhere = pl.BlockSpec(memory_space=pl.ANY)
+    anywhere = pl.BlockSpec(memory_space=pltpu.HBM)
     cols = 2 * NZ
     own = users // cols
     sems = pltpu.SemaphoreType.DMA
@@ -426,6 +425,7 @@
         scratch_shapes=[
             pltpu.VMEM((UNITS, tile_len, HALF), jnp.bfloat16),
             pltpu.VMEM((OBS, NX, NY * rows, R), jnp.bfloat16),
+            pltpu.VMEM((OBS, NX, R, NY * rows), jnp.bfloat16),
             pltpu.VMEM((OBS, NX, users, NY * rows), jnp.float32),
             pltpu.VMEM((OBS, NX, users, NY * rows), jnp.bfloat16),
             pltpu.VMEM((ITERS, users, R), jnp.float32),
@@ -447,9 +447,21 @@
         + [sems((ITERS,))] * 6
         + [sems((2,))] * 2,
         compiler_params=pltpu.CompilerParams(
-            collective_id=0, has_side_effects=True, vmem_limit_bytes=60 * 1024 * 1024
+            collective_id=0, has_side_effects=True, vmem_limit_bytes=48 * 2**20
         ),
-    )(tile_counts, observed_tiles, confidence.reshape(1, users), previous, flat, item_factors)
+    )(
+        *(
+            pltpu.with_memory_space_constraint(array, pltpu.HBM)
+            for array in (
+                tile_counts,
+                observed_tiles,
+                confidence.reshape(1, users),
+                previous,
+                flat,
+                item_factors,
+            )
+        )
+    )
 
 
 def solution(mesh):

time: 90.6 us -> 88.2 us (0.974)
  Pallas kernels: 88.9 us -> 87.5 us
  local copies, waits for them, and re-layouts: 1.57 us -> 0.66 us
    pallas_call x1, Pallas kernels: 88.9 us -> 87.5 us  [local(): pl.pallas_call(functools.partial(kernel, events=events, rows=rows), out_s...]
    unnamed x1, local copies, waits for them, and re-layouts: 1.57 us -> 0.66 us
where the time goes in v3:
time: 88.2 us; the launch traced here: 88.1 us
  Pallas kernels  87.5 us (99%)
    pallas_call x1, Pallas kernels, local(): pl.pallas_call(functools.partial(kernel, events=events, rows=rows), out_s...  87.5 us

profile of v3, /device:TPU:1, one launch (start us, length us, event | category | flops | bytes accessed | tf_op | source)
XLA Modules:
  0.0 88.1 jit_solution(3134668598536515637)
XLA Ops:
  0.0 87.5 %shard_map.64 = f32[128,256]{1,0:T(8,128)S(1)} custom-call(s32[4]{0:T(128)} %counts_hbm.1, s32[1,2]{1,0:T(1,128)} %observed_hbm.1, f32[1,128]{1,0:T(1,128)} %bitcast.7, bf16[128,256]{1,0:T(8,128)(2,1)} %prev_hbm.1, s32[512,128]{1,0:T(8,128)} %bitcast.6, bf16[4,64,256]{2,1,0:T(8,128)(2,1)} %item_hbm.1), custom_call_target="tpu_custom_call" | custom-call | tf_op jit(solution)/shard_map/pallas_call | solution.py:420
  87.5 0.7 copy.9

commit v4 on v3

--- a/solution.py
+++ b/solution.py
@@ -105,6 +105,7 @@
     steps,
     dots,
     gram,
+    gram_other,
     counts,
     observed,
     conf_in,
@@ -119,6 +120,9 @@
     high_recv,
     low_send,
     low_recv,
+    late_send,
+    late_recv,
+    gram_sem,
     step_sem,
     dot_sem,
     *,
@@ -140,11 +144,15 @@
     def base_row(row):
         return pl.multiple_of(row * rows, rows)
 
+    partner = my_z * 2 + (1 - my_core)
     peers = []
+    same = []
+    cross = []
     for dz in sorted(range(NZ), key=lambda d: -min(d, NZ - d)):
         for flip in (0, 1):
             if dz or flip:
                 peers.append(((my_z + dz) % NZ) * 2 + (my_core + flip) % 2)
+                (cross if flip else same).append(peers[-1])
 
     mine = base_row(me_row)
     barrier = pltpu.get_barrier_semaphore()
@@ -279,12 +287,13 @@
     for index, (piece, _, _) in enumerate(events[1:]):
         _, axis, sign, _, dx, _, _, _, stride = piece
         done[(-dx - (sign * stride if axis == "x" else 0)) % NX] = index
+    passed = max(index for index, (_, follow, _) in enumerate(events[1:]) if follow)
     for index, (piece, follow, _) in enumerate(events[1:]):
         copy_of(piece).wait_recv()
         for other in follow:
             copy_of(other).start()
         for dx in range(NX):
-            if done[dx] == index:
+            if max(done[dx], passed) == index:
                 first_pass((my_x + dx) % NX)
 
     waits = []
@@ -292,8 +301,8 @@
     def finish(ref, sem):
         pltpu.make_async_copy(ref, ref, sem).wait()
 
-    def to_peers(place, send, recv):
-        for col in peers:
+    def to_peers(place, send, recv, those):
+        for col in those:
             pltpu.make_async_remote_copy(
                 src_ref=place.at[me_col],
                 dst_ref=place.at[me_col],
@@ -302,17 +311,17 @@
                 device_id=(me_row, col),
                 device_id_type=MESH,
             ).start()
-        waits.append((place.at[pl.ds(0, cols - 1)], send))
-
-    def with_gram(vector):
+        waits.append((place.at[pl.ds(0, len(those))], send))
+
+    def with_gram(vector, matrix):
         return jnp.dot(
             vector,
-            gram[...],
+            matrix,
             precision=lax.Precision.HIGHEST,
             preferred_element_type=jnp.float32,
         )
 
-    def exchange_sums(k):
+    def send_sums(k):
         for col in peers:
             pltpu.make_async_remote_copy(
                 src_ref=part.at[k, pl.ds(pl.multiple_of(col * own, own), own), :],
@@ -323,9 +332,10 @@
                 device_id_type=MESH,
             ).start()
         heard[k, me_col] = part[k, pl.ds(pl.multiple_of(me_col * own, own), own), :]
-        several = heard.at[k, pl.ds(0, cols - 1)]
-        waits.append((several, sum_send.at[k]))
-        finish(several, sum_recv.at[k])
+        waits.append((heard.at[k, pl.ds(0, cols - 1)], sum_send.at[k]))
+
+    def take_sums(k):
+        finish(heard.at[k, pl.ds(0, cols - 1)], sum_recv.at[k])
         total = heard[k, 0]
         for col in range(1, cols):
             total = total + heard[k, col]
@@ -335,13 +345,25 @@
         return ref[k].astype(jnp.float32).reshape(users, R)
 
     start = prev_in[...].astype(jnp.float32)
-    part[0] = part[0] - with_gram(start)
+    part[0] = part[0] - with_gram(start, gram[...])
     mine_users = (
         lax.broadcasted_iota(jnp.int32, (own, users), 1)
         == me_col * own + lax.broadcasted_iota(jnp.int32, (own, users), 0)
     ).astype(jnp.float32).astype(jnp.bfloat16)
+    send_sums(0)
+    trade = pltpu.make_async_remote_copy(
+        src_ref=gram,
+        dst_ref=gram_other,
+        send_sem=gram_sem.at[0],
+        recv_sem=gram_sem.at[1],
+        device_id=(me_row, partner),
+        device_id_type=MESH,
+    )
+    trade.start()
     ours = jnp.dot(mine_users, prev_in[...], preferred_element_type=jnp.float32)
-    residual = exchange_sums(0) - RIDGE * ours
+    trade.wait_recv()
+    gram_both = gram[...] + gram_other[...]
+    residual = take_sums(0) - RIDGE * ours
     direction = residual
     norm_now = jnp.sum(residual * residual, axis=1, keepdims=True)
     lane = lax.broadcasted_iota(jnp.int32, (own, HALF), 1)
@@ -351,26 +373,41 @@
         rest = (direction - top.astype(jnp.float32)).astype(jnp.bfloat16)
         high[k, me_col] = top
         low[k, me_col] = rest
-        to_peers(high.at[k], high_send.at[k], high_recv.at[k])
-        to_peers(low.at[k], low_send.at[k], low_recv.at[k])
-        if k == ITERS - 1:
+        to_peers(high.at[k], high_send.at[k], high_recv.at[k], peers)
+        if k < ITERS - 1:
+            to_peers(low.at[k], low_send.at[k], low_recv.at[k], same)
+        else:
             steps[me_col] = jnp.where(lane == k, norm_now, scalars)
-            to_peers(steps, step_sem.at[0], step_sem.at[1])
+            to_peers(steps, step_sem.at[0], step_sem.at[1], peers)
+            to_peers(low.at[k], low_send.at[k], low_recv.at[k], same)
+            to_peers(low.at[k], late_send.at[k], late_recv.at[k], cross)
         direction = top.astype(jnp.float32) + rest.astype(jnp.float32)
         finish(high.at[k, pl.ds(0, cols - 1)], high_recv.at[k])
         upper = whole(high, k)
         rounded = upper.astype(jnp.bfloat16)
+        if k == ITERS - 1:
+            break
         sums = jnp.zeros((users, R), jnp.float32)
         for s in range(OBS):
             for chunk in range(NX):
                 sums = sums + weighted(rounded, s, chunk)
-        finish(low.at[k, pl.ds(0, cols - 1)], low_recv.at[k])
-        vector = upper + whole(low, k)
-        sums = sums + with_gram(vector)
-        if k == ITERS - 1:
-            break
-        part[k + 1] = sums
-        image = exchange_sums(k + 1) + RIDGE * direction
+        place = part.at[k + 1]
+        place[...] = sums
+        finish(low.at[k, pl.ds(0, len(same))], low_recv.at[k])
+        parity = [2 * z + my_core for z in range(NZ)]
+        vector = jnp.concatenate(
+            [
+                high[k, col].astype(jnp.float32) + low[k, col].astype(jnp.float32)
+                for col in parity
+            ],
+            axis=0,
+        )
+        applied = with_gram(vector, gram_both)
+        for z, col in enumerate(parity):
+            place[pl.ds(pl.multiple_of(col * own, own), own), :] += applied[z * own : (z + 1) * own]
+        send_sums(k + 1)
+        to_peers(low.at[k], late_send.at[k], late_recv.at[k], cross)
+        image = take_sums(k + 1) + RIDGE * direction
         step_size = norm_now / jnp.sum(direction * image, axis=1, keepdims=True)
         scalars = jnp.where(lane == k, step_size, scalars)
         residual = residual - step_size * image
@@ -378,17 +415,29 @@
         direction = residual + (norm_next / norm_now) * direction
         norm_now = norm_next
 
-    dot_here = jnp.sum(sums * vector, axis=1, keepdims=True)
+    terms = jnp.zeros((users, span), jnp.float32)
+    for s in range(OBS):
+        for chunk in range(NX):
+            scores = jnp.dot(rounded, turned[s, chunk], preferred_element_type=jnp.float32)
+            weights = (cs[s, chunk] * scores).astype(jnp.bfloat16)
+            terms = terms + weights.astype(jnp.float32) * scores
+    dot_here = jnp.sum(terms, axis=1, keepdims=True) + jnp.sum(
+        with_gram(upper, gram[...]) * upper, axis=1, keepdims=True
+    )
     dots[me_col] = jnp.broadcast_to(
         jnp.sum(jnp.where(eye, dot_here, 0.0), axis=0, keepdims=True), (8, users)
     )
-    to_peers(dots, dot_sem.at[0], dot_sem.at[1])
+    to_peers(dots, dot_sem.at[0], dot_sem.at[1], peers)
     finish(steps.at[pl.ds(0, cols - 1)], step_sem.at[1])
+    finish(low.at[ITERS - 1, pl.ds(0, len(same))], low_recv.at[ITERS - 1])
+    for k in range(ITERS):
+        finish(low.at[k, pl.ds(0, len(cross))], late_recv.at[k])
+    vector = upper + whole(low, ITERS - 1)
     known = steps[...].reshape(users, HALF)
     answer = start
     for k in range(ITERS - 1):
         answer = answer + known[:, k : k + 1] * (whole(high, k) + whole(low, k))
-    ridge = RIDGE * jnp.sum(vector * vector, axis=1, keepdims=True)
+    ridge = RIDGE * jnp.sum(upper * upper, axis=1, keepdims=True)
     finish(dots.at[pl.ds(0, cols - 1)], dot_sem.at[1])
     total = dots[0, 0:1]
     for col in range(1, cols):
@@ -398,6 +447,7 @@
 
     for piece in copies:
         copies[piece].wait_send()
+    trade.wait_send()
     for several, sem in waits:
         finish(several, sem)
 
@@ -435,6 +485,7 @@
             pltpu.VMEM((cols, own, HALF), jnp.float32),
             pltpu.VMEM((cols, 8, users), jnp.float32),
             pltpu.VMEM((R, R), jnp.float32),
+            pltpu.VMEM((R, R), jnp.float32),
             pltpu.SMEM(tile_counts.shape, jnp.int32),
             pltpu.SMEM(observed_tiles.shape, jnp.int32),
             pltpu.VMEM((1, users), jnp.float32),
@@ -444,8 +495,8 @@
             sems((messages,)),
             sems((messages,)),
         ]
-        + [sems((ITERS,))] * 6
-        + [sems((2,))] * 2,
+        + [sems((ITERS,))] * 8
+        + [sems((2,))] * 3,
         compiler_params=pltpu.CompilerParams(
             collective_id=0, has_side_effects=True, vmem_limit_bytes=48 * 2**20
         ),

time: 88.2 us -> 86.2 us (0.977)
  Pallas kernels: 87.5 us -> 85.5 us
    pallas_call x1, Pallas kernels: 87.5 us -> 85.5 us  [local(): pl.pallas_call(functools.partial(kernel, events=events, rows=rows), out_s...]
where the time goes in v4:
time: 86.2 us; the launch traced here: 86.1 us
  Pallas kernels  85.5 us (99%)
    pallas_call x1, Pallas kernels, local(): pl.pallas_call(functools.partial(kernel, events=events, rows=rows), out_s...  85.5 us

profile of v4, /device:TPU:1, one launch (start us, length us, event | category | flops | bytes accessed | tf_op | source)
XLA Modules:
  0.0 86.1 jit_solution(15475736614796173217)
XLA Ops:
  0.0 85.5 %shard_map.64 = f32[128,256]{1,0:T(8,128)S(1)} custom-call(s32[4]{0:T(128)} %counts_hbm.1, s32[1,2]{1,0:T(1,128)} %observed_hbm.1, f32[1,128]{1,0:T(1,128)} %bitcast.7, bf16[128,256]{1,0:T(8,128)(2,1)} %prev_hbm.1, s32[512,128]{1,0:T(8,128)} %bitcast.6, bf16[4,64,256]{2,1,0:T(8,128)(2,1)} %item_hbm.1), custom_call_target="tpu_custom_call" | custom-call | tf_op jit(solution)/shard_map/pallas_call | solution.py:470
  85.5 0.7 copy.9

commit v5 on v4

--- a/solution.py
+++ b/solution.py
@@ -174,7 +174,7 @@
     others = []
     for i, (src, dst) in enumerate(
         (
-            (words_hbm, words_in),
+            (words_hbm, words_in.at[pl.ds(0, words_hbm.shape[0]), :]),
             (counts_hbm, counts),
             (observed_hbm, observed),
             (conf_hbm, conf_in),
@@ -217,7 +217,7 @@
 
     def expand():
         conf = column(conf_in[...])
-        words_wide = words_in.shape[1]
+        words_tall, words_wide = words_hbm.shape
         lanes = 8 * words_wide
         word_of = lax.broadcasted_iota(jnp.int32, (words_wide, lanes), 0)
         slot_of = lax.broadcasted_iota(jnp.int32, (words_wide, lanes), 1)
@@ -225,8 +225,8 @@
         spreader = jnp.where((slot_of >> 3) == word_of, scale, 0.0).astype(jnp.bfloat16)
         for s in range(OBS):
             count = counts[observed[0, s]]
-            for half in range(words_in.shape[0] // (users * OBS)):
-                words = words_in[pl.ds(half * OBS + s, users, stride=words_in.shape[0] // users), :]
+            for half in range(words_tall // (users * OBS)):
+                words = words_in[pl.ds(half * OBS + s, users, stride=words_tall // users), :]
                 shifted = jnp.dot(
                     words.astype(jnp.float32).astype(jnp.bfloat16),
                     spreader,
@@ -321,6 +321,18 @@
             preferred_element_type=jnp.float32,
         )
 
+    def in_parts(rounded, parts):
+        return sum(
+            jnp.dot(rounded, part_now, preferred_element_type=jnp.float32) for part_now in parts
+        )
+
+    def parts_of(matrix):
+        parts = []
+        for _ in range(3):
+            parts.append(matrix.astype(jnp.bfloat16))
+            matrix = matrix - parts[-1].astype(jnp.float32)
+        return parts[::-1]
+
     def send_sums(k):
         for col in peers:
             pltpu.make_async_remote_copy(
@@ -345,7 +357,8 @@
         return ref[k].astype(jnp.float32).reshape(users, R)
 
     start = prev_in[...].astype(jnp.float32)
-    part[0] = part[0] - with_gram(start, gram[...])
+    gram_parts = parts_of(gram[...])
+    part[0] = part[0] - in_parts(prev_in[...], gram_parts)
     mine_users = (
         lax.broadcasted_iota(jnp.int32, (own, users), 1)
         == me_col * own + lax.broadcasted_iota(jnp.int32, (own, users), 0)
@@ -422,7 +435,7 @@
             weights = (cs[s, chunk] * scores).astype(jnp.bfloat16)
             terms = terms + weights.astype(jnp.float32) * scores
     dot_here = jnp.sum(terms, axis=1, keepdims=True) + jnp.sum(
-        with_gram(upper, gram[...]) * upper, axis=1, keepdims=True
+        in_parts(rounded, gram_parts) * upper, axis=1, keepdims=True
     )
     dots[me_col] = jnp.broadcast_to(
         jnp.sum(jnp.where(eye, dot_here, 0.0), axis=0, keepdims=True), (8, users)
@@ -490,7 +503,7 @@
             pltpu.SMEM(observed_tiles.shape, jnp.int32),
             pltpu.VMEM((1, users), jnp.float32),
             pltpu.VMEM((users, R), jnp.bfloat16),
-            pltpu.VMEM(flat.shape, jnp.int32),
+            pltpu.VMEM((flat.shape[0] + 8, HALF), jnp.int32),
             sems((7,)),
             sems((messages,)),
             sems((messages,)),

time: 86.2 us -> 86 us (level)
  no operation moved by 1% of the time
where the time goes in v5:
time: 86 us; the launch traced here: 85.9 us
  Pallas kernels  85.3 us (99%)
    pallas_call x1, Pallas kernels, local(): pl.pallas_call(functools.partial(kernel, events=events, rows=rows), out_s...  85.3 us

profile of v5, /device:TPU:1, one launch (start us, length us, event | category | flops | bytes accessed | tf_op | source)
XLA Modules:
  0.0 85.9 jit_solution(4189190481895439915)
XLA Ops:
  0.0 85.3 %shard_map.64 = f32[128,256]{1,0:T(8,128)S(1)} custom-call(s32[4]{0:T(128)} %counts_hbm.1, s32[1,2]{1,0:T(1,128)} %observed_hbm.1, f32[1,128]{1,0:T(1,128)} %bitcast.7, bf16[128,256]{1,0:T(8,128)(2,1)} %prev_hbm.1, s32[512,128]{1,0:T(8,128)} %bitcast.6, bf16[4,64,256]{2,1,0:T(8,128)(2,1)} %item_hbm.1), custom_call_target="tpu_custom_call" | custom-call | tf_op jit(solution)/shard_map/pallas_call | solution.py:483
  85.3 0.7 copy.9

commit v6 on v5

--- a/solution.py
+++ b/solution.py
@@ -393,7 +393,8 @@
             steps[me_col] = jnp.where(lane == k, norm_now, scalars)
             to_peers(steps, step_sem.at[0], step_sem.at[1], peers)
             to_peers(low.at[k], low_send.at[k], low_recv.at[k], same)
-            to_peers(low.at[k], late_send.at[k], late_recv.at[k], cross)
+            for past in range(ITERS):
+                to_peers(low.at[past], late_send.at[past], late_recv.at[past], cross)
         direction = top.astype(jnp.float32) + rest.astype(jnp.float32)
         finish(high.at[k, pl.ds(0, cols - 1)], high_recv.at[k])
         upper = whole(high, k)
@@ -419,7 +420,6 @@
         for z, col in enumerate(parity):
             place[pl.ds(pl.multiple_of(col * own, own), own), :] += applied[z * own : (z + 1) * own]
         send_sums(k + 1)
-        to_peers(low.at[k], late_send.at[k], late_recv.at[k], cross)
         image = take_sums(k + 1) + RIDGE * direction
         step_size = norm_now / jnp.sum(direction * image, axis=1, keepdims=True)
         scalars = jnp.where(lane == k, step_size, scalars)

time: 86 us -> 85.9 us (level)
  no operation moved by 1% of the time
where the time goes in v6:
time: 85.9 us; the launch traced here: 85.8 us
  Pallas kernels  85.1 us (99%)
    pallas_call x1, Pallas kernels, local(): pl.pallas_call(functools.partial(kernel, events=events, rows=rows), out_s...  85.1 us

profile of v6, /device:TPU:1, one launch (start us, length us, event | category | flops | bytes accessed | tf_op | source)
XLA Modules:
  0.0 85.8 jit_solution(4547800331659912379)
XLA Ops:
  0.0 85.1 %shard_map.64 = f32[128,256]{1,0:T(8,128)S(1)} custom-call(s32[4]{0:T(128)} %counts_hbm.1, s32[1,2]{1,0:T(1,128)} %observed_hbm.1, f32[1,128]{1,0:T(1,128)} %bitcast.7, bf16[128,256]{1,0:T(8,128)(2,1)} %prev_hbm.1, s32[512,128]{1,0:T(8,128)} %bitcast.6, bf16[4,64,256]{2,1,0:T(8,128)(2,1)} %item_hbm.1), custom_call_target="tpu_custom_call" | custom-call | tf_op jit(solution)/shard_map/pallas_call | solution.py:483
  85.1 0.7 copy.9
